TPU v7x, 256 devices: a whole 4x4x8 slice. The times are simulated.
256 devices in a mesh: dp: 4 (over x), ep: 64 (over y, z, core).
Axes of the slice: x: 4, y: 4, z: 8, core: 2. Of those that a mesh axis runs over, the one named last changes fastest.
Arguments:
- tokens: bfloat16 [32768, 2048], P(('dp', 'ep'))
- cotangent: bfloat16 [32768, 2048], P(('dp', 'ep'))
- expert_ids: int32 [32768, 8], P(('dp', 'ep')), may hold values from 0 to 63, all different within a row; in each aligned block of 128 rows (0 to 127, 128 to 255, ...) at most 18 rows name the same one
- route_weights: bfloat16 [32768, 8], P(('dp', 'ep')), may hold values from 0.029907227 to 0.3984375
- weights: bfloat16 [64, 3, 2048, 384], P('ep')
- first_moment: bfloat16 [64, 3, 2048, 384], P('ep', None, 'dp'), may hold values from -4 to 4
- second_moment: bfloat16 [64, 3, 2048, 384], P('ep', None, 'dp'), may hold values from 0.049804688 to 0.5
Outputs:
- token_grad: bfloat16 [32768, 2048], P(('dp', 'ep'))
- routing_grad: bfloat16 [32768, 8], P(('dp', 'ep'))
- new_first: bfloat16 [64, 3, 2048, 384], P('ep', None, 'dp')
- new_second: bfloat16 [64, 3, 2048, 384], P('ep', None, 'dp')
- update: bfloat16 [64, 3, 2048, 384], P('ep', None, 'dp')
Inputs may be any that keep to these rules, and one draw needn't show every extreme that they name: `expert_ids`: among the 128 rows of one device no expert is named by more than 18 rows.
All inputs are finite; a program needn't handle non-finite values.
Results may differ from a plain program's by a relative error of at most 0.0057.
Values may be sent and summed in bfloat16 or wider, within the bound.
No kernel may reach another device: no remote copies, remote signals or barrier semaphores. Data moves between devices by JAX's collectives and lax.ppermute only.
A program may use at most 128 MiB of HBM per device.

v0:
```python
import jax
import jax.numpy as jnp
from jax import lax
from jax.experimental.layout import Layout, with_layout_constraint
from jax.sharding import Mesh, PartitionSpec as P

ADAM_STEP = 10
CORES = 2
BF16 = jnp.bfloat16
F32 = jnp.float32
INFO = 128


def plane(mesh):
    dp, ep = mesh.devices.shape
    y = 4
    z = ep // (y * CORES)
    return Mesh(mesh.devices.reshape(dp, y, z, CORES), ("x", "y", "z", "c"))


def on_device(tokens, cotangent, expert_ids, route_weights, weights, first_moment, second_moment):
    tok_count, model_width = tokens.shape
    topk_count = expert_ids.shape[1]
    hidden_units = weights.shape[3]
    ny, nz, nc = (lax.axis_size("y"), lax.axis_size("z"), lax.axis_size("c"))
    experts = ny * nz * nc
    capacity = (tok_count * topk_count * 9 + 8 * experts - 1) // (8 * experts)
    dests = ny * nc
    slots = nz * capacity
    yi, zi, ci = (lax.axis_index("y"), lax.axis_index("z"), lax.axis_index("c"))
    me = ((yi * nz + zi) * nc + ci).astype(F32)
    info = jnp.concatenate([expert_ids.astype(BF16), route_weights], 1)
    info = jnp.pad(info, ((0, 0), (0, INFO - 2 * topk_count)))
    info = with_layout_constraint(info, Layout((0, 1)))
    rows = with_layout_constraint(jnp.concatenate([tokens, info], 1), Layout((0, 1)))
    all_x = lax.all_gather(rows, "z", axis=0, tiled=True)
    all_cot = lax.all_gather(cotangent, "z", axis=0, tiled=True)
    ids = all_x[:, model_width : model_width + topk_count].astype(F32)
    dest = jnp.arange(dests, dtype=jnp.int32)
    dest_expert = ((dest // nc * nz + zi) * nc + dest % nc).astype(F32)
    match = jnp.any(ids[:, :, None] == dest_expert[None, None, :], 1)
    tri = jnp.tril(jnp.ones((tok_count, tok_count), BF16))
    count = jnp.einsum(
        "ab,sbd->sad",
        tri,
        match.astype(BF16).reshape(nz, tok_count, dests),
        preferred_element_type=F32,
    )
    base = (jnp.arange(nz, dtype=jnp.int32) * capacity - 1).astype(F32)[:, None, None]
    slot = jnp.where(match, (count + base).reshape(nz * tok_count, dests), -1.0)
    slot = lax.optimization_barrier(slot.T)
    picks = (
        slot[:, None, :] == jnp.arange(slots, dtype=jnp.int32).astype(F32)[None, :, None]
    ).astype(BF16)
    picks = lax.optimization_barrier(picks.reshape(dests * slots, nz * tok_count))

    def exchange(rows):
        width = rows.shape[1]
        out = lax.all_to_all(
            rows.reshape(dests, slots, width), ("y", "c"), split_axis=0, concat_axis=0, tiled=True
        )
        return out.reshape(dests * slots, width)

    recv = exchange(jnp.dot(picks, all_x, preferred_element_type=F32).astype(BF16))
    recv_cot = exchange(jnp.dot(picks, all_cot, preferred_element_type=F32).astype(BF16))
    recv_x = recv[:, :model_width]
    recv_ids = recv[:, model_width : model_width + topk_count].astype(F32)
    recv_rw = recv[:, model_width + topk_count : model_width + 2 * topk_count].astype(F32)
    mine = recv_ids == me
    row_weight = jnp.sum(jnp.where(mine, recv_rw, 0.0), 1, keepdims=True)
    w_gate, w_up, w_down = (weights[0, 0], weights[0, 1], weights[0, 2])
    gate_val = jnp.dot(recv_x, w_gate, preferred_element_type=F32)
    up_val = jnp.dot(recv_x, w_up, preferred_element_type=F32)
    sigmoid_gate = jax.nn.sigmoid(gate_val)
    activated = gate_val * sigmoid_gate
    hidden = lax.optimization_barrier((activated * up_val).astype(BF16))
    back_val = jnp.dot(recv_cot, w_down, preferred_element_type=F32)
    route_part = jnp.sum(hidden.astype(F32) * back_val, 1, keepdims=True).astype(BF16)
    scaled = row_weight * back_val
    dgate = (scaled * up_val * sigmoid_gate * (1.0 + gate_val * (1.0 - sigmoid_gate))).astype(BF16)
    dup = (scaled * activated).astype(BF16)
    down_cot = (row_weight * recv_cot.astype(F32)).astype(BF16)
    slot_back = jnp.einsum("rh,dh->rd", dgate, w_gate, preferred_element_type=F32)
    slot_back = slot_back + jnp.einsum("rh,dh->rd", dup, w_up, preferred_element_type=F32)
    route_rows = jnp.where(mine, route_part, jnp.zeros((), BF16))
    route_rows = jnp.pad(route_rows, ((0, 0), (0, INFO - topk_count)))
    send_back = jnp.concatenate([slot_back.astype(BF16), route_rows], 1)
    send_back, grad_x, grad_cot = lax.optimization_barrier((send_back, recv_x, down_cot))
    back_rows = exchange(send_back)
    partial = lax.dot_general(
        picks, back_rows, (((0,), (0,)), ((), ())), preferred_element_type=F32
    )
    total = lax.psum_scatter(partial.astype(BF16), "z", scatter_dimension=0, tiled=True)
    token_grad = total[:, :model_width]
    routing_grad = total[:, model_width : model_width + topk_count]
    grad_local = jnp.stack(
        [
            jnp.einsum("rd,rh->dh", grad_x, dgate, preferred_element_type=F32).astype(BF16),
            jnp.einsum("rd,rh->dh", grad_x, dup, preferred_element_type=F32).astype(BF16),
            jnp.einsum("rd,rh->dh", grad_cot, hidden, preferred_element_type=F32).astype(BF16),
        ],
        0,
    )
    grad_share = lax.psum_scatter(grad_local, "x", scatter_dimension=1, tiled=True).astype(F32)[
        None
    ]
    square = jnp.sum(grad_share * grad_share)
    square = jnp.broadcast_to(square, (experts, 1, 128))
    square = lax.all_to_all(square, ("y", "z", "c"), split_axis=0, concat_axis=0, tiled=True)
    square_sum = lax.psum(jnp.sum(square[:, 0, 0]), "x")
    param_count = 3.0 * experts * model_width * hidden_units
    root_mean = jnp.sqrt(square_sum / param_count + 1e-06)
    clip_factor = jnp.minimum(1.0, 0.5 / root_mean)
    clipped = clip_factor * grad_share
    first_next = 0.9 * first_moment.astype(F32) + 0.1 * clipped
    second_next = 0.95 * second_moment.astype(F32) + 0.05 * clipped * clipped
    update = (
        first_next
        / (1.0 - 0.9**ADAM_STEP)
        / (jnp.sqrt(second_next / (1.0 - 0.95**ADAM_STEP)) + 1e-08)
    )
    return (
        token_grad,
        routing_grad,
        first_next.astype(BF16),
        second_next.astype(BF16),
        update.astype(BF16),
    )


def solution(mesh):
    tok = P(("x", "y", "z", "c"), None)
    ep = ("y", "z", "c")
    state = P(ep, None, "x", None)
    return jax.shard_map(
        on_device,
        mesh=plane(mesh),
        in_specs=(tok, tok, tok, tok, P(ep, None, None, None), state, state),
        out_specs=(tok, tok, state, state, state),
        check_vma=False,
    )
```

profile of v0, /device:TPU:1, one launch (start us, length us, event | category | flops | bytes accessed | tf_op | source)
XLA Modules:
  0.0 375.6 jit_solution(4099123066367515721)
XLA Ops:
  7.2 0.0 all-gather.3.cloned.1.call-start
  7.2 0.7 convert_element_type.110
  7.9 0.7 pad_maximum_fusion.1
  8.6 0.1 copy.53
  8.7 1.9 fusion.34
  10.6 0.0 all-gather.3.cloned.1.call-update
  10.6 0.0 all-gather.5.cloned.1.call-start
  10.7 0.7 all-gather.5.cloned.1.call-update
  11.4 0.1 eq.47
  11.5 60.1 %all-gather.3.cloned.1.call-done = bf16[1024,2176]{1,0:T(8,128)(2,1)} async-done(((bf16[128,2176]{1,0:T(8,128)(2,1)}), bf16[1024,2176]{1,0:T(8,128)(2,1)}) %all-gather.3.cloned.1.call-update) | async-done | bytes 4456464 | tf_op jit(solution)/shard_map/all_gather | solution.py:36
  71.6 1.0 slice_convert_fusion
  72.6 0.2 copy.54
  72.8 0.1 compare_reduce_fusion
  72.9 0.1 fusion.33
  73.0 0.5 fusion.3
  73.5 9.6 %convolution_convert_fusion = bf16[1152,2176]{1,0:T(8,128)(2,1)} fusion(bf16[1152,1024]{1,0:T(8,128)(2,1)S(1)} %fusion.3, bf16[1024,2176]{1,0:T(8,128)(2,1)} %all-gather.3.cloned.1.call-done), kind=kOutput, calls=%fused_computation | convolution fusion | flops 5136334848 | bytes 11829248 | tf_op jit(solution)/shard_map/dot_general | solution.py:64
  83.1 5.3 %all-to-all-start = ((bf16[8,144,2176]{2,1,0:T(8,128)(2,1)}), bf16[8,144,2176]{2,1,0:T(8,128)(2,1)}, u32[]{:S(2)}, u32[]{:S(2)}) async-start(bf16[8,144,2176]{2,1,0:T(8,128)(2,1)} %bitcast.80), calls=%async_computation | async-start | bytes 10027008 | tf_op jit(solution)/shard_map/all_to_all | solution.py:59
  88.5 38.3 %all-gather.5.cloned.1.call-done = bf16[1024,2048]{1,0:T(8,128)(2,1)} async-done(((bf16[128,2048]{1,0:T(8,128)(2,1)}), bf16[1024,2048]{1,0:T(8,128)(2,1)}) %all-gather.5.cloned.1.call-update) | async-done | bytes 4194320 | tf_op jit(solution)/shard_map/all_gather | solution.py:37
  126.8 8.8 %convolution_convert_fusion.1 = bf16[1152,2048]{1,0:T(8,128)(2,1)} fusion(bf16[1152,1024]{1,0:T(8,128)(2,1)S(1)} %fusion.3, bf16[1024,2048]{1,0:T(8,128)(2,1)} %all-gather.5.cloned.1.call-done), kind=kOutput, calls=%fused_computation.6 | convolution fusion | flops 4834197504 | bytes 11272192 | tf_op jit(solution)/shard_map/dot_general | solution.py:65
  135.6 10.4 %all-to-all-done = bf16[8,144,2176]{2,1,0:T(8,128)(2,1)} async-done(((bf16[8,144,2176]{2,1,0:T(8,128)(2,1)}), bf16[8,144,2176]{2,1,0:T(8,128)(2,1)}, u32[]{:S(2)}, u32[]{:S(2)}) %all-to-all-start) | async-done | bytes 5013536 | tf_op jit(solution)/shard_map/all_to_all | solution.py:59
  146.0 5.4 %all-to-all-start.1 = ((bf16[8,144,2048]{2,1,0:T(8,128)(2,1)}), bf16[8,144,2048]{2,1,0:T(8,128)(2,1)}, u32[]{:S(2)}, u32[]{:S(2)}) async-start(bf16[8,144,2048]{2,1,0:T(8,128)(2,1)} %bitcast.82), calls=%async_computation.1 | async-start | bytes 9437184 | tf_op jit(solution)/shard_map/all_to_all | solution.py:59
  151.5 0.0 reduce-scatter.5.cloned.1.call-start
  151.5 5.3 %slice.43 = bf16[1152,2048]{1,0:T(8,128)(2,1)} slice(bf16[1152,2176]{1,0:T(8,128)(2,1)} %bitcast.7), slice={[0:1152], [0:2048]} | slice | bytes 9437184 | tf_op jit(solution)/shard_map/slice | solution.py:66
  156.8 1.4 select_reduce_fusion
  158.1 6.4 %fusion.19 = f32[1152,384]{0,1:T(8,128)} fusion(bf16[1,3,2048,384]{3,2,1,0:T(8,128)(2,1)} %param.11, bf16[1152,2176]{1,0:T(8,128)(2,1)} %bitcast.7), kind=kOutput, calls=%fused_computation.39 | convolution fusion | flops 1811939328 | bytes 8060928 | tf_op jit(solution)/shard_map/dot_general | solution.py:73
  164.5 6.3 %fusion.16 = f32[1152,384]{0,1:T(8,128)} fusion(bf16[1,3,2048,384]{3,2,1,0:T(8,128)(2,1)} %param.11, bf16[1152,2176]{1,0:T(8,128)(2,1)} %bitcast.7), kind=kOutput, calls=%fused_computation.36 | convolution fusion | flops 1811939328 | bytes 8060928 | tf_op jit(solution)/shard_map/dot_general | solution.py:72
  170.8 35.1 %all-to-all-done.1 = bf16[8,144,2048]{2,1,0:T(8,128)(2,1)} async-done(((bf16[8,144,2048]{2,1,0:T(8,128)(2,1)}), bf16[8,144,2048]{2,1,0:T(8,128)(2,1)}, u32[]{:S(2)}, u32[]{:S(2)}) %all-to-all-start.1) | async-done | bytes 4718624 | tf_op jit(solution)/shard_map/all_to_all | solution.py:59
  205.9 7.9 %multiply_convert_fusion.2 = (bf16[1152,384]{0,1:T(8,128)(2,1)}, bf16[1152,384]{0,1:T(8,128)(2,1)S(1)}, bf16[1152,384]{0,1:T(8,128)(2,1)S(1)}, f32[1152,384]{0,1:T(8,128)S(1)}) fusion(f32[1152]{0:T(1024)S(1)} %select_reduce_fusion, f32[1152,384]{0,1:T(8,128)} %fusion.16, f32[1152,384]{0,1:T(8,128)} %fusion.19, bf16[1152,2048]{1,0:T(8,128)(2,1)} %bitcast.9, ...), kind=kOutput, calls=%fused_computation.30 | convolution fusion | flops 1819017216 | bytes 14258688 | tf_op jit(solution)/shard_map/dot_general | solution.py:77
  213.8 0.2 multiply_reduce_fusion
  214.0 1.2 broadcast_select_fusion
  215.3 0.0 slice-done.2
  215.3 0.0 slice-done.3
  215.3 2.7 fusion.14
  218.0 0.0 copy-done.2
  218.0 0.0 slice-start
  218.0 4.5 %fusion.1 = bf16[1152,2048]{1,0:T(8,128)(2,1)S(1)} fusion(f32[1152,2048]{1,0:T(8,128)S(1)} %fusion.14, bf16[1152,384]{0,1:T(8,128)(2,1)} %get-tuple-element.41, bf16[1,3,2048,384]{3,2,1,0:T(8,128)(2,1)S(1)} %bitcast.86), kind=kOutput, calls=%fused_computation.5 | convolution fusion | flops 1816657920 | bytes 16613376 | tf_op jit(solution)/shard_map/rh,dh->rd/dot_general | solution.py:84
  222.5 0.0 slice-start.1
  222.5 2.7 fusion.2
  225.2 3.2 multiply_convert_fusion
  228.4 0.0 slice-done
  228.5 0.0 slice-done.1
  228.5 0.0 copy-done.4
  228.5 2.8 fusion.6
  231.3 0.0 copy-start.3
  231.3 2.8 fusion.5
  234.2 0.0 copy-done.3
  234.2 2.8 fusion.7
  237.0 2.5 pad_maximum_fusion
  239.5 0.0 reduce-scatter.5.cloned.1.call-update
  239.5 0.0 reduce-scatter.3.cloned.1.call-start
  239.6 62.5 %all_to_all.20 = bf16[8,144,2176]{2,1,0:T(8,128)(2,1)S(1)} all-to-all(bf16[8,144,2176]{2,1,0:T(8,128)(2,1)} %bitcast.79), channel_id=1, replica_groups=mesh['x'=4,'y'=4,'z'=8,'c'=2] {'y','c'}, dimensions={0} | all-to-all | bytes 10027008 | tf_op jit(solution)/shard_map/all_to_all | solution.py:59
  302.1 7.9 %convolution_convert_fusion.2 = bf16[1024,2176]{1,0:T(8,128)(2,1)} fusion(bf16[1152,1024]{1,0:T(8,128)(2,1)S(1)} %fusion.3, bf16[1152,2176]{1,0:T(8,128)(2,1)S(1)} %bitcast.81), kind=kOutput, calls=%fused_computation.7 | convolution fusion | flops 5136056320 | bytes 11829248 | tf_op jit(solution)/shard_map/dot_general | solution.py:90
  310.0 0.0 reduce-scatter.3.cloned.1.call-update
  310.0 0.0 reduce-scatter.5.cloned.1.call-done
  310.0 2.6 fusion.10
  312.7 0.7 broadcast_in_dim.44
  313.3 15.9 %all_to_all.21 = f32[64,1,128]{2,1,0:T(1,128)S(1)} all-to-all(f32[64,1,128]{2,1,0:T(1,128)S(1)} %broadcast_in_dim.44), channel_id=1, replica_groups=mesh['x'=4,'y'=4,'z'=8,'c'=2] {'y','z','c'}, dimensions={0} | all-to-all | bytes 65536 | tf_op jit(solution)/shard_map/all_to_all | solution.py:109
  329.2 0.7 slice_reduce_fusion
  329.9 9.8 %psum.7 = f32[]{:T(128)} all-reduce(f32[]{:T(128)} %slice_reduce_fusion), channel_id=1, replica_groups=mesh['x'=4,'y'=4,'z'=8,'c'=2] {'x'}, use_global_device_ids=true, to_apply=%region_7.8 | all-reduce | flops 1 | bytes 8 | tf_op jit(solution)/shard_map/psum | solution.py:110
  340.4 4.8 %divide_convert_fusion = (bf16[1,3,512,384]{3,2,1,0:T(8,128)(2,1)}, bf16[1,3,512,384]{3,2,1,0:T(8,128)(2,1)}, bf16[1,3,512,384]{3,2,1,0:T(8,128)(2,1)}) fusion(bf16[3,512,384]{2,1,0:T(8,128)(2,1)} %reduce-scatter.5.cloned.1.call-done, bf16[1,3,512,384]{3,2,1,0:T(8,128)(2,1)S(1)} %copy-done, bf16[1,3,512,384]{3,2,1,0:T(8,128)(2,1)S(1)} %copy-done.1, f32[]{:T(128)S(6)} %min.3), kind=kLoop, calls=%fused_computation.27 | loop fusion | flops 10616832 | bytes 7077892 | tf_op jit(solution)/shard_map/convert_element_type | solution.py:127
  345.3 20.6 %reduce-scatter.3.cloned.1.call-done = bf16[128,2176]{1,0:T(8,128)(2,1)} async-done(((bf16[1024,2176]{1,0:T(8,128)(2,1)}), bf16[128,2176]{1,0:T(8,128)(2,1)}) %reduce-scatter.3.cloned.1.call-update) | async-done | bytes 557072 | tf_op jit(solution)/shard_map/reduce_scatter | solution.py:93
  365.8 0.8 slice.45
  366.6 0.7 copy.61
  367.2 1.9 slice.44
  (14 shorter events, 0.0 us)
Async XLA Ops:
  7.2 64.5 %all-gather.3.cloned.1.call-start = ((), (), s32[]{:S(2)}) async-start(), calls=%async_computation.6 | async-start | bytes 5013504 | tf_op jit(solution)/shard_map/all_gather | solution.py:36
  10.6 116.2 %all-gather.5.cloned.1.call-start = ((), (), s32[]{:S(2)}) async-start(), calls=%async_computation.7 | async-start | bytes 4718592 | tf_op jit(solution)/shard_map/all_gather | solution.py:37
  83.1 62.9 %all-to-all-start = ((bf16[8,144,2176]{2,1,0:T(8,128)(2,1)}), bf16[8,144,2176]{2,1,0:T(8,128)(2,1)}, u32[]{:S(2)}, u32[]{:S(2)}) async-start(bf16[8,144,2176]{2,1,0:T(8,128)(2,1)} %bitcast.80), calls=%async_computation | async-start | bytes 10027008 | tf_op jit(solution)/shard_map/all_to_all | solution.py:59
  146.0 59.9 %all-to-all-start.1 = ((bf16[8,144,2048]{2,1,0:T(8,128)(2,1)}), bf16[8,144,2048]{2,1,0:T(8,128)(2,1)}, u32[]{:S(2)}, u32[]{:S(2)}) async-start(bf16[8,144,2048]{2,1,0:T(8,128)(2,1)} %bitcast.82), calls=%async_computation.1 | async-start | bytes 9437184 | tf_op jit(solution)/shard_map/all_to_all | solution.py:59
  151.5 158.5 %reduce-scatter.5.cloned.1.call-start = ((), (), s32[]{:S(2)}) async-start(), calls=%async_computation.9 | async-start | bytes 5898240 | tf_op jit(solution)/shard_map/reduce_scatter | solution.py:104
  205.9 9.4 %slice-start.2 = ((s8[4718592]{0:T(1024)(128)(4,1)}), s8[4194304]{0:T(1024)(128)(4,1)S(1)}, s32[]{:S(2)}) async-start(s8[4718592]{0:T(1024)(128)(4,1)} %bitcast.85), calls=%async_computation.12 | async-start | bytes 8388608
  205.9 9.4 %slice-start.3 = ((s8[4718592]{0:T(1024)(128)(4,1)}), s8[524288]{0:T(1024)(128)(4,1)S(1)}, s32[]{:S(2)}) async-start(s8[4718592]{0:T(1024)(128)(4,1)} %bitcast.85), calls=%async_computation.13 | async-start | bytes 1048576
  213.8 4.2 %copy-start.2 = (bf16[1152,384]{0,1:T(8,128)(2,1)}, bf16[1152,384]{0,1:T(8,128)(2,1)S(1)}, u32[]{:S(2)}) copy-start(bf16[1152,384]{0,1:T(8,128)(2,1)S(1)} %get-tuple-element.43) | copy-start | bytes 2654212
  218.0 10.5 %slice-start = ((s8[4718592]{0:T(1024)(128)(4,1)}), s8[4194304]{0:T(1024)(128)(4,1)S(1)}, s32[]{:S(2)}) async-start(s8[4718592]{0:T(1024)(128)(4,1)} %bitcast.83), calls=%async_computation.10 | async-start | bytes 8388608
  222.5 6.0 %slice-start.1 = ((s8[4718592]{0:T(1024)(128)(4,1)}), s8[524288]{0:T(1024)(128)(4,1)S(1)}, s32[]{:S(2)}) async-start(s8[4718592]{0:T(1024)(128)(4,1)} %bitcast.83), calls=%async_computation.11 | async-start | bytes 1048576
  225.2 3.3 copy-start.4
  231.3 2.8 copy-start.3
  239.5 126.3 %reduce-scatter.3.cloned.1.call-start = ((), (), s32[]{:S(2)}) async-start(), calls=%async_computation.8 | async-start | bytes 5013504 | tf_op jit(solution)/shard_map/reduce_scatter | solution.py:93
  310.0 30.5 %copy-start = (bf16[1,3,512,384]{3,2,1,0:T(8,128)(2,1)S(1)}, bf16[1,3,512,384]{3,2,1,0:T(8,128)(2,1)}, u32[]{:S(2)}) copy-start(bf16[1,3,512,384]{3,2,1,0:T(8,128)(2,1)} %param.13) | copy-start | bytes 3538948
  310.0 30.5 %copy-start.1 = (bf16[1,3,512,384]{3,2,1,0:T(8,128)(2,1)S(1)}, bf16[1,3,512,384]{3,2,1,0:T(8,128)(2,1)}, u32[]{:S(2)}) copy-start(bf16[1,3,512,384]{3,2,1,0:T(8,128)(2,1)} %param.12) | copy-start | bytes 3538948
Sparse Core Ops, SparseCore 0:
  10.7 60.8 all-gather.2
  73.4 53.3 all-gather.4
  239.6 50.6 reduce-scatter.4
  310.1 55.6 reduce-scatter.2
where the time goes:
time: 376 us
  waiting for transfers between devices  165 us (44%)
  blocking collectives  88.2 us (23%)
  matrix products  62.5 us (17%)
  other arithmetic  24.3 us (6%)
  between operations  14.7 us (4%)
  starting transfers between devices  10.9 us (3%)
  local copies, waits for them, and re-layouts  9.63 us (3%)
    all_to_all x1, blocking collectives, exchange(): lax.all_to_all(rows.reshape(dests, slots, width), ('y', 'c'), split_axis=...  62.5 us
    all_gather x1, waiting for transfers between devices, on_device(): all_x = lax.all_gather(rows, 'z', axis=0, tiled=True)  60.1 us
    all_to_all x2, waiting for transfers between devices, exchange(): lax.all_to_all(rows.reshape(dests, slots, width), ('y', 'c'), split_axis=...  45.6 us
    all_gather x1, waiting for transfers between devices, on_device(): all_cot = lax.all_gather(cotangent, 'z', axis=0, tiled=True)  38.3 us
    reduce_scatter x1, waiting for transfers between devices, on_device(): lax.psum_scatter(partial.astype(BF16), 'z', scatter_dimension=0, tiled=True)  20.6 us
    all_to_all x1, blocking collectives, on_device(): lax.all_to_all(square, ('y', 'z', 'c'), split_axis=0, concat_axis=0, tile...  15.9 us
    all_to_all x2, starting transfers between devices, exchange(): lax.all_to_all(rows.reshape(dests, slots, width), ('y', 'c'), split_axis=...  10.8 us
    psum x1, blocking collectives, on_device(): square_sum = lax.psum(jnp.sum(square[:, 0, 0]), 'x')  9.81 us
  transfers between devices with their start and end apart: 6, of which 5 were waited for; matrix products, arithmetic and copies ran while one was open for 15% of the time, Pallas kernels for 0%

commit v1 on v0

--- a/solution.py
+++ b/solution.py
@@ -33,8 +33,11 @@
     info = jnp.pad(info, ((0, 0), (0, INFO - 2 * topk_count)))
     info = with_layout_constraint(info, Layout((0, 1)))
     rows = with_layout_constraint(jnp.concatenate([tokens, info], 1), Layout((0, 1)))
-    all_x = lax.all_gather(rows, "z", axis=0, tiled=True)
-    all_cot = lax.all_gather(cotangent, "z", axis=0, tiled=True)
+    all_x, all_cot = jnp.split(
+        lax.all_gather(jnp.concatenate([rows, cotangent], axis=1), "z", axis=0, tiled=True),
+        [rows.shape[1]],
+        axis=1,
+    )
     ids = all_x[:, model_width : model_width + topk_count].astype(F32)
     dest = jnp.arange(dests, dtype=jnp.int32)
     dest_expert = ((dest // nc * nz + zi) * nc + dest % nc).astype(F32)

time: 376 us -> 416 us (1.11)
  waiting for transfers between devices: 165 us -> 205 us
    all_to_all x2, waiting for transfers between devices: 45.6 us -> 83.9 us  [exchange(): lax.all_to_all(rows.reshape(dests, slots, width), ('y', 'c'), split_axis=...]
    all_gather x2 -> x1, waiting for transfers between devices: 98.4 us -> 100 us  [on_device(): lax.all_gather(jnp.concatenate([rows, cotangent], axis=1), 'z', axis=0, t...]
  transfers between devices with their start and end apart: 6 -> 5, of which waited for: 5 -> 4; matrix products, arithmetic and copies ran while one was open for 15% -> 11% of each run, Pallas kernels for 0% -> 0%
where the time goes in v1:
time: 416 us; the launch traced here: 415 us
  waiting for transfers between devices  205 us (49%)
  blocking collectives  88.2 us (21%)
  matrix products  62.5 us (15%)
  other arithmetic  24.7 us (6%)
  between operations  14.7 us (4%)
  starting transfers between devices  10.9 us (3%)
  local copies, waits for them, and re-layouts  9.65 us (2%)
    all_gather x1, waiting for transfers between devices, on_device(): lax.all_gather(jnp.concatenate([rows, cotangent], axis=1), 'z', axis=0, t...  100 us
    all_to_all x2, waiting for transfers between devices, exchange(): lax.all_to_all(rows.reshape(dests, slots, width), ('y', 'c'), split_axis=...  83.9 us
    all_to_all x1, blocking collectives, exchange(): lax.all_to_all(rows.reshape(dests, slots, width), ('y', 'c'), split_axis=...  62.5 us
    reduce_scatter x1, waiting for transfers between devices, on_device(): lax.psum_scatter(partial.astype(BF16), 'z', scatter_dimension=0, tiled=True)  20.5 us
    all_to_all x1, blocking collectives, on_device(): lax.all_to_all(square, ('y', 'z', 'c'), split_axis=0, concat_axis=0, tile...  15.9 us
    all_to_all x2, starting transfers between devices, exchange(): lax.all_to_all(rows.reshape(dests, slots, width), ('y', 'c'), split_axis=...  10.8 us
    psum x1, blocking collectives, on_device(): square_sum = lax.psum(jnp.sum(square[:, 0, 0]), 'x')  9.8 us
    dot_general x1, matrix products, on_device(): jnp.dot(picks, all_x, preferred_element_type=F32).astype(BF16)  9.59 us
  transfers between devices with their start and end apart: 5, of which 4 were waited for; matrix products, arithmetic and copies ran while one was open for 11% of the time, Pallas kernels for 0%

profile of v1, /device:TPU:1, one launch (start us, length us, event | category | flops | bytes accessed | tf_op | source)
XLA Modules:
  0.0 415.3 jit_solution(8228125467404579501)
XLA Ops:
  7.2 0.0 all-gather.2.cloned.1.call-start
  7.2 0.7 convert_element_type.110
  7.9 0.7 pad_maximum_fusion.1
  8.6 0.1 copy.53
  8.7 2.3 fusion.38
  11.0 0.0 all-gather.2.cloned.1.call-update
  11.0 0.1 eq.47
  11.1 100.2 %all-gather.2.cloned.1.call-done = bf16[1024,4224]{1,0:T(8,128)(2,1)} async-done(((bf16[128,4224]{1,0:T(8,128)(2,1)}), bf16[1024,4224]{1,0:T(8,128)(2,1)}) %all-gather.2.cloned.1.call-update) | async-done | bytes 8650768 | tf_op jit(solution)/shard_map/all_gather | solution.py:37
  111.3 1.0 slice_convert_fusion
  112.3 0.2 copy.54
  112.5 0.1 compare_reduce_fusion
  112.6 0.1 fusion.36
  112.7 0.5 fusion.3
  113.2 9.6 %convolution_convert_fusion = bf16[1152,2176]{1,0:T(8,128)(2,1)} fusion(bf16[1152,1024]{1,0:T(8,128)(2,1)S(1)} %fusion.3, bf16[1024,4224]{1,0:T(8,128)(2,1)} %all-gather.2.cloned.1.call-done), kind=kOutput, calls=%fused_computation | convolution fusion | flops 5136334848 | bytes 11829248 | tf_op jit(solution)/shard_map/dot_general | solution.py:67
  122.8 5.3 %all-to-all-start = ((bf16[8,144,2176]{2,1,0:T(8,128)(2,1)}), bf16[8,144,2176]{2,1,0:T(8,128)(2,1)}, u32[]{:S(2)}, u32[]{:S(2)}) async-start(bf16[8,144,2176]{2,1,0:T(8,128)(2,1)} %bitcast.78), calls=%async_computation | async-start | bytes 10027008 | tf_op jit(solution)/shard_map/all_to_all | solution.py:62
  128.1 8.8 %convolution_convert_fusion.1 = bf16[1152,2048]{1,0:T(8,128)(2,1)} fusion(bf16[1152,1024]{1,0:T(8,128)(2,1)S(1)} %fusion.3, bf16[1024,4224]{1,0:T(8,128)(2,1)} %all-gather.2.cloned.1.call-done), kind=kOutput, calls=%fused_computation.6 | convolution fusion | flops 4834197504 | bytes 11272192 | tf_op jit(solution)/shard_map/dot_general | solution.py:68
  136.9 48.8 %all-to-all-done = bf16[8,144,2176]{2,1,0:T(8,128)(2,1)} async-done(((bf16[8,144,2176]{2,1,0:T(8,128)(2,1)}), bf16[8,144,2176]{2,1,0:T(8,128)(2,1)}, u32[]{:S(2)}, u32[]{:S(2)}) %all-to-all-start) | async-done | bytes 5013536 | tf_op jit(solution)/shard_map/all_to_all | solution.py:62
  185.7 5.4 %all-to-all-start.1 = ((bf16[8,144,2048]{2,1,0:T(8,128)(2,1)}), bf16[8,144,2048]{2,1,0:T(8,128)(2,1)}, u32[]{:S(2)}, u32[]{:S(2)}) async-start(bf16[8,144,2048]{2,1,0:T(8,128)(2,1)} %bitcast.80), calls=%async_computation.1 | async-start | bytes 9437184 | tf_op jit(solution)/shard_map/all_to_all | solution.py:62
  191.2 0.0 reduce-scatter.5.cloned.1.call-start
  191.2 5.3 %slice.44 = bf16[1152,2048]{1,0:T(8,128)(2,1)} slice(bf16[1152,2176]{1,0:T(8,128)(2,1)} %bitcast.7), slice={[0:1152], [0:2048]} | slice | bytes 9437184 | tf_op jit(solution)/shard_map/slice | solution.py:69
  196.5 1.4 select_reduce_fusion
  197.8 6.3 %fusion.23 = f32[1152,384]{0,1:T(8,128)} fusion(bf16[1,3,2048,384]{3,2,1,0:T(8,128)(2,1)} %param.11, bf16[1152,2176]{1,0:T(8,128)(2,1)} %bitcast.7), kind=kOutput, calls=%fused_computation.45 | convolution fusion | flops 1811939328 | bytes 8060928 | tf_op jit(solution)/shard_map/dot_general | solution.py:76
  204.2 6.3 %fusion.20 = f32[1152,384]{0,1:T(8,128)} fusion(bf16[1,3,2048,384]{3,2,1,0:T(8,128)(2,1)} %param.11, bf16[1152,2176]{1,0:T(8,128)(2,1)} %bitcast.7), kind=kOutput, calls=%fused_computation.42 | convolution fusion | flops 1811939328 | bytes 8060928 | tf_op jit(solution)/shard_map/dot_general | solution.py:75
  210.5 35.1 %all-to-all-done.1 = bf16[8,144,2048]{2,1,0:T(8,128)(2,1)} async-done(((bf16[8,144,2048]{2,1,0:T(8,128)(2,1)}), bf16[8,144,2048]{2,1,0:T(8,128)(2,1)}, u32[]{:S(2)}, u32[]{:S(2)}) %all-to-all-start.1) | async-done | bytes 4718624 | tf_op jit(solution)/shard_map/all_to_all | solution.py:62
  245.6 0.0 slice-start.2
  245.6 7.9 %multiply_convert_fusion.2 = (bf16[1152,384]{0,1:T(8,128)(2,1)}, bf16[1152,384]{0,1:T(8,128)(2,1)S(1)}, bf16[1152,384]{0,1:T(8,128)(2,1)S(1)}, f32[1152,384]{0,1:T(8,128)S(1)}) fusion(f32[1152]{0:T(1024)S(1)} %select_reduce_fusion, f32[1152,384]{0,1:T(8,128)} %fusion.20, f32[1152,384]{0,1:T(8,128)} %fusion.23, bf16[1152,2048]{1,0:T(8,128)(2,1)} %bitcast.9, ...), kind=kOutput, calls=%fused_computation.36 | convolution fusion | flops 1819017216 | bytes 14258688 | tf_op jit(solution)/shard_map/dot_general | solution.py:80
  253.5 0.2 multiply_reduce_fusion
  253.7 1.2 broadcast_select_fusion
  255.0 0.0 slice-done.2
  255.0 0.0 slice-done.3
  255.0 2.7 fusion.18
  257.6 0.0 copy-done.2
  257.7 0.0 slice-start
  257.7 4.5 %fusion.1 = bf16[1152,2048]{1,0:T(8,128)(2,1)S(1)} fusion(f32[1152,2048]{1,0:T(8,128)S(1)} %fusion.18, bf16[1152,384]{0,1:T(8,128)(2,1)} %get-tuple-element.41, bf16[1,3,2048,384]{3,2,1,0:T(8,128)(2,1)S(1)} %bitcast.84), kind=kOutput, calls=%fused_computation.5 | convolution fusion | flops 1816657920 | bytes 16613376 | tf_op jit(solution)/shard_map/rh,dh->rd/dot_general | solution.py:87
  262.1 0.0 slice-start.1
  262.2 2.7 fusion.2
  264.9 3.2 multiply_convert_fusion
  268.1 0.0 slice-done
  268.1 0.0 slice-done.1
  268.1 0.0 copy-done.4
  268.2 2.8 fusion.8
  271.0 0.0 copy-start.3
  271.0 2.8 fusion.7
  273.8 0.0 copy-done.3
  273.8 2.8 fusion.9
  276.7 2.5 pad_maximum_fusion
  279.1 0.0 reduce-scatter.5.cloned.1.call-update
  279.2 0.0 reduce-scatter.3.cloned.1.call-start
  279.2 62.5 %all_to_all.20 = bf16[8,144,2176]{2,1,0:T(8,128)(2,1)S(1)} all-to-all(bf16[8,144,2176]{2,1,0:T(8,128)(2,1)} %bitcast.77), channel_id=1, replica_groups=mesh['x'=4,'y'=4,'z'=8,'c'=2] {'y','c'}, dimensions={0} | all-to-all | bytes 10027008 | tf_op jit(solution)/shard_map/all_to_all | solution.py:62
  341.7 7.9 %convolution_convert_fusion.2 = bf16[1024,2176]{1,0:T(8,128)(2,1)} fusion(bf16[1152,1024]{1,0:T(8,128)(2,1)S(1)} %fusion.3, bf16[1152,2176]{1,0:T(8,128)(2,1)S(1)} %bitcast.79), kind=kOutput, calls=%fused_computation.7 | convolution fusion | flops 5136056320 | bytes 11829248 | tf_op jit(solution)/shard_map/dot_general | solution.py:93
  349.6 0.0 reduce-scatter.3.cloned.1.call-update
  349.7 0.0 reduce-scatter.5.cloned.1.call-done
  349.7 2.6 fusion.12
  352.3 0.7 broadcast_in_dim.44
  353.0 15.9 %all_to_all.21 = f32[64,1,128]{2,1,0:T(1,128)S(1)} all-to-all(f32[64,1,128]{2,1,0:T(1,128)S(1)} %broadcast_in_dim.44), channel_id=1, replica_groups=mesh['x'=4,'y'=4,'z'=8,'c'=2] {'y','z','c'}, dimensions={0} | all-to-all | bytes 65536 | tf_op jit(solution)/shard_map/all_to_all | solution.py:112
  368.9 0.7 slice_reduce_fusion
  369.6 9.8 %psum.7 = f32[]{:T(128)} all-reduce(f32[]{:T(128)} %slice_reduce_fusion), channel_id=1, replica_groups=mesh['x'=4,'y'=4,'z'=8,'c'=2] {'x'}, use_global_device_ids=true, to_apply=%region_7.8 | all-reduce | flops 1 | bytes 8 | tf_op jit(solution)/shard_map/psum | solution.py:113
  380.1 0.0 copy-done
  380.1 0.0 copy-done.1
  380.1 4.8 %divide_convert_fusion = (bf16[1,3,512,384]{3,2,1,0:T(8,128)(2,1)}, bf16[1,3,512,384]{3,2,1,0:T(8,128)(2,1)}, bf16[1,3,512,384]{3,2,1,0:T(8,128)(2,1)}) fusion(bf16[3,512,384]{2,1,0:T(8,128)(2,1)} %reduce-scatter.5.cloned.1.call-done, bf16[1,3,512,384]{3,2,1,0:T(8,128)(2,1)S(1)} %copy-done, bf16[1,3,512,384]{3,2,1,0:T(8,128)(2,1)S(1)} %copy-done.1, f32[]{:T(128)S(6)} %min.3), kind=kLoop, calls=%fused_computation.31 | loop fusion | flops 10616832 | bytes 7077892 | tf_op jit(solution)/shard_map/convert_element_type | solution.py:130
  384.9 20.5 %reduce-scatter.3.cloned.1.call-done = bf16[128,2176]{1,0:T(8,128)(2,1)} async-done(((bf16[1024,2176]{1,0:T(8,128)(2,1)}), bf16[128,2176]{1,0:T(8,128)(2,1)}) %reduce-scatter.3.cloned.1.call-update) | async-done | bytes 557072 | tf_op jit(solution)/shard_map/reduce_scatter | solution.py:96
  405.5 0.8 slice.46
  406.2 0.7 copy.61
  406.9 1.9 slice.45
  (11 shorter events, 0.0 us)
Async XLA Ops:
  7.2 104.1 %all-gather.2.cloned.1.call-start = ((), (), s32[]{:S(2)}) async-start(), calls=%async_computation.6 | async-start | bytes 9732096 | tf_op jit(solution)/shard_map/all_gather | solution.py:37
  122.8 62.9 %all-to-all-start = ((bf16[8,144,2176]{2,1,0:T(8,128)(2,1)}), bf16[8,144,2176]{2,1,0:T(8,128)(2,1)}, u32[]{:S(2)}, u32[]{:S(2)}) async-start(bf16[8,144,2176]{2,1,0:T(8,128)(2,1)} %bitcast.78), calls=%async_computation | async-start | bytes 10027008 | tf_op jit(solution)/shard_map/all_to_all | solution.py:62
  185.7 59.9 %all-to-all-start.1 = ((bf16[8,144,2048]{2,1,0:T(8,128)(2,1)}), bf16[8,144,2048]{2,1,0:T(8,128)(2,1)}, u32[]{:S(2)}, u32[]{:S(2)}) async-start(bf16[8,144,2048]{2,1,0:T(8,128)(2,1)} %bitcast.80), calls=%async_computation.1 | async-start | bytes 9437184 | tf_op jit(solution)/shard_map/all_to_all | solution.py:62
  191.2 158.5 %reduce-scatter.5.cloned.1.call-start = ((), (), s32[]{:S(2)}) async-start(), calls=%async_computation.8 | async-start | bytes 5898240 | tf_op jit(solution)/shard_map/reduce_scatter | solution.py:107
  245.6 9.4 %slice-start.2 = ((s8[4718592]{0:T(1024)(128)(4,1)}), s8[4194304]{0:T(1024)(128)(4,1)S(1)}, s32[]{:S(2)}) async-start(s8[4718592]{0:T(1024)(128)(4,1)} %bitcast.83), calls=%async_computation.11 | async-start | bytes 8388608
  245.6 9.4 %slice-start.3 = ((s8[4718592]{0:T(1024)(128)(4,1)}), s8[524288]{0:T(1024)(128)(4,1)S(1)}, s32[]{:S(2)}) async-start(s8[4718592]{0:T(1024)(128)(4,1)} %bitcast.83), calls=%async_computation.12 | async-start | bytes 1048576
  253.5 4.2 %copy-start.2 = (bf16[1152,384]{0,1:T(8,128)(2,1)}, bf16[1152,384]{0,1:T(8,128)(2,1)S(1)}, u32[]{:S(2)}) copy-start(bf16[1152,384]{0,1:T(8,128)(2,1)S(1)} %get-tuple-element.43) | copy-start | bytes 2654212
  257.7 10.5 %slice-start = ((s8[4718592]{0:T(1024)(128)(4,1)}), s8[4194304]{0:T(1024)(128)(4,1)S(1)}, s32[]{:S(2)}) async-start(s8[4718592]{0:T(1024)(128)(4,1)} %bitcast.81), calls=%async_computation.9 | async-start | bytes 8388608
  262.1 6.0 %slice-start.1 = ((s8[4718592]{0:T(1024)(128)(4,1)}), s8[524288]{0:T(1024)(128)(4,1)S(1)}, s32[]{:S(2)}) async-start(s8[4718592]{0:T(1024)(128)(4,1)} %bitcast.81), calls=%async_computation.10 | async-start | bytes 1048576
  264.9 3.3 copy-start.4
  271.0 2.8 copy-start.3
  279.2 126.3 %reduce-scatter.3.cloned.1.call-start = ((), (), s32[]{:S(2)}) async-start(), calls=%async_computation.7 | async-start | bytes 5013504 | tf_op jit(solution)/shard_map/reduce_scatter | solution.py:96
  349.6 30.5 %copy-start = (bf16[1,3,512,384]{3,2,1,0:T(8,128)(2,1)S(1)}, bf16[1,3,512,384]{3,2,1,0:T(8,128)(2,1)}, u32[]{:S(2)}) copy-start(bf16[1,3,512,384]{3,2,1,0:T(8,128)(2,1)} %param.13) | copy-start | bytes 3538948
  349.6 30.5 %copy-start.1 = (bf16[1,3,512,384]{3,2,1,0:T(8,128)(2,1)S(1)}, bf16[1,3,512,384]{3,2,1,0:T(8,128)(2,1)}, u32[]{:S(2)}) copy-start(bf16[1,3,512,384]{3,2,1,0:T(8,128)(2,1)} %param.12) | copy-start | bytes 3538948
Sparse Core Ops, SparseCore 0:
  11.1 100.1 all-gather.1
  279.3 50.6 reduce-scatter.4
  349.8 55.6 reduce-scatter.2
